TPU v7x, 512 devices: a whole 4x8x8 slice. The times are simulated.
512 devices in a mesh: leaf: 64 (over y, x, core), panel: 8 (over z).
Axes of the slice: x: 4, y: 8, z: 8, core: 2. Of those that a mesh axis runs over, the one named last changes fastest.
Arguments:
- rhs_0: bfloat16 [4096, 1024], P('leaf', 'panel'), may hold values from -6 to 6
- rhs_1: bfloat16 [4096, 1024], P('leaf', 'panel'), may hold values from -6 to 6
- rhs_2: bfloat16 [4096, 1024], P('leaf', 'panel'), may hold values from -6 to 6
- rhs_3: bfloat16 [4096, 1024], P('leaf', 'panel'), may hold values from -6 to 6
- inv_0: bfloat16 [4096, 4096], P(('leaf', 'panel')), as said below
- inv_1: bfloat16 [4096, 2048], P(('leaf', 'panel')), as said below
- inv_2: bfloat16 [4096, 1024], P(('leaf', 'panel')), as said below
- inv_3: bfloat16 [4096, 512], P(('leaf', 'panel')), as said below
- coupling_1: bfloat16 [4096, 2048], P(('leaf', 'panel')), may hold values from -0.125 to 0.125
- coupling_2: bfloat16 [4096, 1024], P(('leaf', 'panel')), may hold values from -0.1875 to 0.1875
- coupling_3: bfloat16 [4096, 512], P(('leaf', 'panel')), may hold values from -0.25 to 0.25
- update_rows_1: int32 [2, 2048], replicated, may hold values from 0 to 4095, as said below
- update_rows_2: int32 [4, 1024], replicated, may hold values from 0 to 6143, as said below
- update_rows_3: int32 [8, 512], replicated, may hold values from 0 to 7167, as said below
Outputs:
- solution_0: bfloat16 [4096, 1024], P('leaf', 'panel')
- solution_1: bfloat16 [4096, 1024], P('leaf', 'panel')
- solution_2: bfloat16 [4096, 1024], P('leaf', 'panel')
- solution_3: bfloat16 [4096, 1024], P('leaf', 'panel')
Inputs may be any that keep to these rules, and one draw needn't show every extreme that they name: `update_rows_1`: row f lists the update rows of front f of depth 1: 2048 distinct indices into its ancestor rows, holding 0 and the last ancestor row. `update_rows_2`: row f lists the update rows of front f of depth 2: 1024 distinct indices into its ancestor rows, holding 0 and the last ancestor row. `update_rows_3`: row f lists the update rows of front f of depth 3: 512 distinct indices into its ancestor rows, holding 0 and the last ancestor row. `inv_0`: the block is lower triangular with its diagonal between 0.5 and 2. `inv_1`: each 2048-row block is lower triangular with its diagonal between 0.5 and 2. `inv_2`: each 1024-row block is lower triangular with its diagonal between 0.5 and 2. `inv_3`: each 512-row block is lower triangular with its diagonal between 0.5 and 2.
All inputs are finite; a program needn't handle non-finite values.
Results may differ from a plain program's by a relative error of at most 0.014.
Values may be sent and summed in bfloat16 or wider, within the bound.
No kernel may reach another device: no remote copies, remote signals or barrier semaphores. Data moves between devices by JAX's collectives and lax.ppermute only.
A program may use at most 64 MiB of HBM per device.

v0:
```python
import jax
import jax.numpy as jnp
from jax import lax
from jax.sharding import PartitionSpec as P

PIVOTS = 4096
LEVELS = 4


def swapped(value, axis, bit):
    mask = 2**bit
    pairs = [(source, source ^ mask) for source in range(lax.axis_size(axis))]
    return lax.ppermute(value, axis, pairs)


def collect_rows(own_block, groups, front_rows):
    gathered = lax.all_gather(own_block, "leaf", axis=0, tiled=True)
    row_start = lax.axis_index("leaf") // groups * front_rows
    return lax.dynamic_slice_in_dim(gathered, row_start, front_rows, 0)


def halve_sums(block, groups):
    my_index = lax.axis_index("leaf")
    for bit_pos in reversed(range(groups.bit_length() - 1)):
        half_rows = block.shape[0] // 2
        lower_half = block[:half_rows]
        upper_half = block[half_rows:]
        is_high = my_index >> bit_pos & 1 == 1
        keep_part = jnp.where(is_high, upper_half, lower_half)
        send_part = jnp.where(is_high, lower_half, upper_half)
        block = keep_part + swapped(send_part, "leaf", bit_pos)
    return block


def reduce_rows(block, groups):
    return halve_sums(block, groups)


def contract_rows(left, right):
    return lax.dot_general(
        left, right, (((0,), (0,)), ((), ())), preferred_element_type=jnp.float32
    )


def body(
    rhs_0,
    rhs_1,
    rhs_2,
    rhs_3,
    inv_0,
    inv_1,
    inv_2,
    inv_3,
    coupling_1,
    coupling_2,
    coupling_3,
    update_rows_1,
    update_rows_2,
    update_rows_3,
):
    rhs_all = [rhs_0, rhs_1, rhs_2, rhs_3]
    lists_all = [None, update_rows_1, update_rows_2, update_rows_3]
    columns = rhs_0.shape[1]
    leaf_count = lax.axis_size("leaf")
    front_sizes = [PIVOTS >> depth_now for depth_now in range(LEVELS)]
    offsets = [0]
    for depth_now in range(1, LEVELS):
        offsets.append(offsets[-1] + front_sizes[depth_now - 1])
    fetched = (
        lax.all_gather(inv_0, "panel", axis=0, tiled=True),
        lax.all_gather(inv_1, "panel", axis=0, tiled=True),
        lax.all_gather(inv_2, "panel", axis=0, tiled=True),
        lax.all_gather(inv_3, "panel", axis=0, tiled=True),
        lax.all_gather(coupling_1, "panel", axis=0, tiled=True),
        lax.all_gather(coupling_2, "panel", axis=0, tiled=True),
        lax.all_gather(coupling_3, "panel", axis=0, tiled=True),
    )
    inv_rows_all = [fetched[0], fetched[1], fetched[2], fetched[3]]
    coup_rows_all = [None, fetched[4], fetched[5], fetched[6]]
    accumulated = jnp.zeros((offsets[LEVELS - 1], columns), jnp.float32)
    forwards = [None] * LEVELS
    for depth_now in reversed(range(LEVELS)):
        groups = leaf_count >> depth_now
        front_rows = front_sizes[depth_now]
        front = lax.axis_index("leaf") // groups
        summed = rhs_all[depth_now].astype(jnp.float32)
        if depth_now < LEVELS - 1:
            summed = summed + reduce_rows(
                accumulated[offsets[depth_now] : offsets[depth_now] + front_rows], groups
            )
        combined = collect_rows(summed.astype(jnp.bfloat16), groups, front_rows)
        values = jnp.dot(
            inv_rows_all[depth_now], combined, preferred_element_type=jnp.float32
        ).astype(jnp.bfloat16)
        forwards[depth_now] = values
        if depth_now > 0:
            update = contract_rows(coup_rows_all[depth_now], values)
            row_list = lax.dynamic_index_in_dim(lists_all[depth_now], front, 0, keepdims=False)
            accumulated = accumulated.at[row_list].add(update)
    anc_values = jnp.zeros((offsets[LEVELS - 1], columns), jnp.bfloat16)
    outputs = []
    for depth_now in range(LEVELS):
        groups = leaf_count >> depth_now
        front_rows = front_sizes[depth_now]
        front = lax.axis_index("leaf") // groups
        if depth_now > 0:
            row_list = lax.dynamic_index_in_dim(lists_all[depth_now], front, 0, keepdims=False)
            picked = jnp.take(anc_values, row_list, axis=0)
            pulled = jnp.dot(coup_rows_all[depth_now], picked, preferred_element_type=jnp.float32)
            adjusted = (forwards[depth_now].astype(jnp.float32) - pulled).astype(jnp.bfloat16)
        else:
            adjusted = forwards[depth_now]
        partial_value = contract_rows(inv_rows_all[depth_now], adjusted)
        solved = reduce_rows(partial_value, groups).astype(jnp.bfloat16)
        outputs.append(solved)
        if depth_now < LEVELS - 1:
            whole_front = collect_rows(solved, groups, front_rows)
            anc_values = anc_values.at[offsets[depth_now] : offsets[depth_now] + front_rows].set(
                whole_front
            )
    return (outputs[0], outputs[1], outputs[2], outputs[3])


def solution(mesh):
    in_specs = (
        P("leaf", "panel"),
        P("leaf", "panel"),
        P("leaf", "panel"),
        P("leaf", "panel"),
        P(("leaf", "panel"), None),
        P(("leaf", "panel"), None),
        P(("leaf", "panel"), None),
        P(("leaf", "panel"), None),
        P(("leaf", "panel"), None),
        P(("leaf", "panel"), None),
        P(("leaf", "panel"), None),
        P(),
        P(),
        P(),
    )
    out_specs = (P("leaf", "panel"), P("leaf", "panel"), P("leaf", "panel"), P("leaf", "panel"))
    return jax.shard_map(body, mesh=mesh, in_specs=in_specs, out_specs=out_specs, check_vma=False)
```

profile of v0, /device:TPU:1, one launch (start us, length us, event | category | flops | bytes accessed | tf_op | source)
XLA Modules:
  0.0 1056.7 jit_solution(4610110368345489924)
XLA Ops:
  8.0 25.9 %all_gather.43 = bf16[64,512]{1,0:T(8,128)(2,1)S(1)} all-gather(bf16[8,512]{1,0:T(8,128)(2,1)} %param.27), channel_id=1, replica_groups=mesh['leaf'=64,'panel'=8] {'panel'}, dimensions={0}, use_global_device_ids=true | all-gather | bytes 73728 | tf_op jit(solution)/shard_map/all_gather | solution.py:73
  33.9 19.2 %all_gather.44 = bf16[64,512]{1,0:T(8,128)(2,1)S(1)} all-gather(bf16[8,512]{1,0:T(8,128)(2,1)} %param.30), channel_id=1, replica_groups=mesh['leaf'=64,'panel'=8] {'panel'}, dimensions={0}, use_global_device_ids=true | all-gather | bytes 73728 | tf_op jit(solution)/shard_map/all_gather | solution.py:76
  54.4 44.7 %all-gather.8.cloned.1.call-done = bf16[4096,128]{1,0:T(8,128)(2,1)} async-done(((bf16[64,128]{1,0:T(8,128)(2,1)}), bf16[4096,128]{1,0:T(8,128)(2,1)}) %all-gather.8.cloned.1.call-update) | async-done | bytes 1048592 | tf_op jit(solution)/shard_map/all_gather | solution.py:17
  101.2 4.2 scatter_custom_fusion
  108.7 7.2 collective-permute-done
  117.1 3.7 collective-permute-start.1
  129.4 5.4 collective-permute-start.3
  136.3 20.5 %all_gather.46 = bf16[64,1024]{1,0:T(8,128)(2,1)S(1)} all-gather(bf16[8,1024]{1,0:T(8,128)(2,1)S(1)} %copy-done.13), channel_id=1, replica_groups=mesh['leaf'=64,'panel'=8] {'panel'}, dimensions={0}, use_global_device_ids=true | all-gather | bytes 147456 | tf_op jit(solution)/shard_map/all_gather | solution.py:72
  156.8 19.3 %all_gather.47 = bf16[64,1024]{1,0:T(8,128)(2,1)S(1)} all-gather(bf16[8,1024]{1,0:T(8,128)(2,1)S(1)} %copy-done.14), channel_id=1, replica_groups=mesh['leaf'=64,'panel'=8] {'panel'}, dimensions={0}, use_global_device_ids=true | all-gather | bytes 147456 | tf_op jit(solution)/shard_map/all_gather | solution.py:75
  177.4 39.1 %all-gather.10.cloned.1.call-done = bf16[4096,128]{1,0:T(8,128)(2,1)} async-done(((bf16[64,128]{1,0:T(8,128)(2,1)}), bf16[4096,128]{1,0:T(8,128)(2,1)}) %all-gather.10.cloned.1.call-update) | async-done | bytes 1048592 | tf_op jit(solution)/shard_map/all_gather | solution.py:17
  218.1 9.3 scatter_fusion
  228.7 3.9 collective-permute-start.4
  232.6 23.9 %collective-permute-done.4 = f32[1024,128]{1,0:T(8,128)S(1)} collective-permute-done((f32[1024,128]{1,0:T(8,128)S(1)}, f32[1024,128]{1,0:T(8,128)S(1)}, u32[]{:S(2)}, u32[]{:S(2)}) %collective-permute-start.4) | collective-permute-done | bytes 524320 | tf_op jit(solution)/shard_map/ppermute | solution.py:13
  259.8 7.3 collective-permute-done.5
  269.9 4.5 collective-permute-done.6
  279.5 5.6 collective-permute-start.8
  286.6 20.6 %all_gather.49 = bf16[64,2048]{1,0:T(8,128)(2,1)S(1)} all-gather(bf16[8,2048]{1,0:T(8,128)(2,1)S(1)} %copy-done.11), channel_id=1, replica_groups=mesh['leaf'=64,'panel'=8] {'panel'}, dimensions={0}, use_global_device_ids=true | all-gather | bytes 294912 | tf_op jit(solution)/shard_map/all_gather | solution.py:71
  307.3 20.0 %all_gather.50 = bf16[64,2048]{1,0:T(8,128)(2,1)S(1)} all-gather(bf16[8,2048]{1,0:T(8,128)(2,1)S(1)} %copy-done.12), channel_id=1, replica_groups=mesh['leaf'=64,'panel'=8] {'panel'}, dimensions={0}, use_global_device_ids=true | all-gather | bytes 294912 | tf_op jit(solution)/shard_map/all_gather | solution.py:74
  327.3 39.1 %all-gather.12.cloned.1.call-done = bf16[4096,128]{1,0:T(8,128)(2,1)} async-done(((bf16[64,128]{1,0:T(8,128)(2,1)}), bf16[4096,128]{1,0:T(8,128)(2,1)}) %all-gather.12.cloned.1.call-update) | async-done | bytes 1048592 | tf_op jit(solution)/shard_map/all_gather | solution.py:17
  368.3 14.2 %scatter_fusion.1 = f32[7168,128]{1,0:T(8,128)} fusion(f32[7168,128]{1,0:T(8,128)} %scatter_fusion, s32[2048]{0:T(1024)S(1)} %bitcast.44, f32[2048,128]{1,0:T(8,128)S(1)} %copy.80), kind=kCustom, calls=%fused_computation.5 | custom fusion | flops 262144 | bytes 3153920 | tf_op jit(solution)/shard_map/scatter-add | solution.py:99
  384.1 4.9 collective-permute-start.9
  388.9 32.4 %collective-permute-done.9 = f32[2048,128]{1,0:T(8,128)S(1)} collective-permute-done((f32[2048,128]{1,0:T(8,128)S(1)}, f32[2048,128]{1,0:T(8,128)S(1)}, u32[]{:S(2)}, u32[]{:S(2)}) %collective-permute-start.9) | collective-permute-done | bytes 1048608 | tf_op jit(solution)/shard_map/ppermute | solution.py:13
  423.1 19.9 %collective-permute-start.10 = (f32[1024,128]{1,0:T(8,128)S(1)}, f32[1024,128]{1,0:T(8,128)S(1)}, u32[]{:S(2)}, u32[]{:S(2)}) collective-permute-start(f32[1024,128]{1,0:T(8,128)S(1)} %slice_select_fusion.4), channel_id=1, source_target_pairs={{0,128},{8,136},{16,144},{24,152},{32,160},{40,168},{48,176},{56,1... | collective-permute-start | bytes 1572872 | tf_op jit(solution)/shard_map/ppermute | solution.py:13
  443.1 23.3 %collective-permute-done.10 = f32[1024,128]{1,0:T(8,128)S(1)} collective-permute-done((f32[1024,128]{1,0:T(8,128)S(1)}, f32[1024,128]{1,0:T(8,128)S(1)}, u32[]{:S(2)}, u32[]{:S(2)}) %collective-permute-start.10) | collective-permute-done | bytes 524320 | tf_op jit(solution)/shard_map/ppermute | solution.py:13
  468.4 7.4 collective-permute-done.11
  488.2 5.5 collective-permute-start.14
  495.3 22.4 %all_gather.52 = bf16[64,4096]{1,0:T(8,128)(2,1)S(1)} all-gather(bf16[8,4096]{1,0:T(8,128)(2,1)S(1)} %copy-done.9), channel_id=1, replica_groups=mesh['leaf'=64,'panel'=8] {'panel'}, dimensions={0}, use_global_device_ids=true | all-gather | bytes 589824 | tf_op jit(solution)/shard_map/all_gather | solution.py:70
  517.7 57.2 %all-gather.14.cloned.1.call-done = bf16[4096,128]{1,0:T(8,128)(2,1)} async-done(((bf16[64,128]{1,0:T(8,128)(2,1)}), bf16[4096,128]{1,0:T(8,128)(2,1)}) %all-gather.14.cloned.1.call-update) | async-done | bytes 1048592 | tf_op jit(solution)/shard_map/all_gather | solution.py:17
  577.0 4.9 collective-permute-start.15
  581.9 32.4 %collective-permute-done.15 = f32[2048,128]{1,0:T(8,128)S(1)} collective-permute-done((f32[2048,128]{1,0:T(8,128)S(1)}, f32[2048,128]{1,0:T(8,128)S(1)}, u32[]{:S(2)}, u32[]{:S(2)}) %collective-permute-start.15) | collective-permute-done | bytes 1048608 | tf_op jit(solution)/shard_map/ppermute | solution.py:13
  614.5 19.9 %collective-permute-start.16 = (f32[1024,128]{1,0:T(8,128)S(1)}, f32[1024,128]{1,0:T(8,128)S(1)}, u32[]{:S(2)}, u32[]{:S(2)}) collective-permute-start(f32[1024,128]{1,0:T(8,128)S(1)} %slice_select_fusion.3), channel_id=1, source_target_pairs={{0,128},{8,136},{16,144},{24,152},{32,160},{40,168},{48,176},{56,1... | collective-permute-start | bytes 1572872 | tf_op jit(solution)/shard_map/ppermute | solution.py:13
  634.4 23.3 %collective-permute-done.16 = f32[1024,128]{1,0:T(8,128)S(1)} collective-permute-done((f32[1024,128]{1,0:T(8,128)S(1)}, f32[1024,128]{1,0:T(8,128)S(1)}, u32[]{:S(2)}, u32[]{:S(2)}) %collective-permute-start.16) | collective-permute-done | bytes 524320 | tf_op jit(solution)/shard_map/ppermute | solution.py:13
  659.8 7.4 collective-permute-done.17
  679.6 5.5 collective-permute-start.20
  687.2 79.0 %all-gather.16.cloned.1.call-done = bf16[4096,128]{1,0:T(8,128)(2,1)} async-done(((bf16[64,128]{1,0:T(8,128)(2,1)}), bf16[4096,128]{1,0:T(8,128)(2,1)}) %all-gather.16.cloned.1.call-update) | async-done | bytes 1048592 | tf_op jit(solution)/shard_map/all_gather | solution.py:17
  767.7 8.0 gather_fusion
  777.6 3.9 collective-permute-start.21
  781.5 23.9 %collective-permute-done.21 = f32[1024,128]{1,0:T(8,128)S(1)} collective-permute-done((f32[1024,128]{1,0:T(8,128)S(1)}, f32[1024,128]{1,0:T(8,128)S(1)}, u32[]{:S(2)}, u32[]{:S(2)}) %collective-permute-start.21) | collective-permute-done | bytes 524320 | tf_op jit(solution)/shard_map/ppermute | solution.py:13
  807.6 7.3 collective-permute-done.22
  817.7 4.5 collective-permute-done.23
  827.3 5.6 collective-permute-start.25
  835.8 78.3 %all-gather.18.cloned.1.call-done = bf16[4096,128]{1,0:T(8,128)(2,1)} async-done(((bf16[64,128]{1,0:T(8,128)(2,1)}), bf16[4096,128]{1,0:T(8,128)(2,1)}) %all-gather.18.cloned.1.call-update) | async-done | bytes 1048592 | tf_op jit(solution)/shard_map/all_gather | solution.py:17
  921.4 7.2 collective-permute-done.26
  941.0 5.4 collective-permute-start.29
  947.8 80.3 %all-gather.20.cloned.1.call-done = bf16[4096,128]{1,0:T(8,128)(2,1)} async-done(((bf16[64,128]{1,0:T(8,128)(2,1)}), bf16[4096,128]{1,0:T(8,128)(2,1)}) %all-gather.20.cloned.1.call-update) | async-done | bytes 1048592 | tf_op jit(solution)/shard_map/all_gather | solution.py:17
  1030.9 3.7 collective-permute-start.30
  1034.7 4.4 collective-permute-done.30
  1044.2 4.2 collective-permute-start.32
  (187 shorter events, 121.6 us)
Async XLA Ops:
  7.2 92.0 %all-gather.8.cloned.1.call-start = ((), (), s32[]{:S(2)}) async-start(), calls=%async_computation | async-start | bytes 1064960 | tf_op jit(solution)/shard_map/all_gather | solution.py:17
  7.9 208.6 %all-gather.10.cloned.1.call-start = ((), (), s32[]{:S(2)}) async-start(), calls=%async_computation.1 | async-start | bytes 1064960 | tf_op jit(solution)/shard_map/all_gather | solution.py:17
  33.9 86.9 %copy-start.2 = (bf16[64,512]{1,0:T(8,128)(2,1)}, bf16[64,512]{1,0:T(8,128)(2,1)S(1)}, u32[]{:S(2)}) copy-start(bf16[64,512]{1,0:T(8,128)(2,1)S(1)} %all_gather.43) | copy-start | bytes 196612
  106.5 9.5 collective-permute-start
  117.1 7.2 collective-permute-start.1
  124.3 5.0 collective-permute-start.2
  129.4 6.2 collective-permute-start.3
  136.2 230.1 %all-gather.12.cloned.1.call-start = ((), (), s32[]{:S(2)}) async-start(), calls=%async_computation.2 | async-start | bytes 1064960 | tf_op jit(solution)/shard_map/all_gather | solution.py:17
  227.4 79.9 %copy-start.12 = (bf16[8,2048]{1,0:T(8,128)(2,1)S(1)}, bf16[8,2048]{1,0:T(8,128)(2,1)}, u32[]{:S(2)}) copy-start(bf16[8,2048]{1,0:T(8,128)(2,1)} %param.28) | copy-start | bytes 98308
  227.4 99.8 %copy-start.21 = (s32[2,2048]{1,0:T(2,128)S(1)}, s32[2,2048]{1,0:T(2,128)}, u32[]{:S(2)}) copy-start(s32[2,2048]{1,0:T(2,128)} %param.31) | copy-start | bytes 49156
  228.7 27.8 %collective-permute-start.4 = (f32[1024,128]{1,0:T(8,128)S(1)}, f32[1024,128]{1,0:T(8,128)S(1)}, u32[]{:S(2)}, u32[]{:S(2)}) collective-permute-start(f32[1024,128]{1,0:T(8,128)S(1)} %slice_select_fusion.5), channel_id=1, source_target_pairs={{0,128},{8,136},{16,144},{24,152},{32,160},{40,168},{48,176},{56,1... | collective-permute-start | bytes 1572872 | tf_op jit(solution)/shard_map/ppermute | solution.py:13
  257.9 9.2 collective-permute-start.5
  267.2 7.2 collective-permute-start.6
  274.5 5.0 collective-permute-start.7
  279.5 6.4 collective-permute-start.8
  286.6 288.4 %all-gather.14.cloned.1.call-start = ((), (), s32[]{:S(2)}) async-start(), calls=%async_computation.3 | async-start | bytes 1064960 | tf_op jit(solution)/shard_map/all_gather | solution.py:17
  384.1 37.3 %collective-permute-start.9 = (f32[2048,128]{1,0:T(8,128)S(1)}, f32[2048,128]{1,0:T(8,128)S(1)}, u32[]{:S(2)}, u32[]{:S(2)}) collective-permute-start(f32[2048,128]{1,0:T(8,128)S(1)} %slice_select_fusion.1), channel_id=1, source_target_pairs={{0,256},{8,264},{16,272},{24,280},{32,288},{40,296},{48,304},{56,3... | collective-permute-start | bytes 3145736 | tf_op jit(solution)/shard_map/ppermute | solution.py:13
  423.0 72.2 %copy-start.9 = (bf16[8,4096]{1,0:T(8,128)(2,1)S(1)}, bf16[8,4096]{1,0:T(8,128)(2,1)}, u32[]{:S(2)}) copy-start(bf16[8,4096]{1,0:T(8,128)(2,1)} %param.24) | copy-start | bytes 196612
  423.1 43.3 %collective-permute-start.10 = (f32[1024,128]{1,0:T(8,128)S(1)}, f32[1024,128]{1,0:T(8,128)S(1)}, u32[]{:S(2)}, u32[]{:S(2)}) collective-permute-start(f32[1024,128]{1,0:T(8,128)S(1)} %slice_select_fusion.4), channel_id=1, source_target_pairs={{0,128},{8,136},{16,144},{24,152},{32,160},{40,168},{48,176},{56,1... | collective-permute-start | bytes 1572872 | tf_op jit(solution)/shard_map/ppermute | solution.py:13
  466.5 9.3 collective-permute-start.11
  475.9 7.2 collective-permute-start.12
  483.1 5.0 collective-permute-start.13
  488.2 6.4 collective-permute-start.14
  495.2 271.0 %all-gather.16.cloned.1.call-start = ((), (), s32[]{:S(2)}) async-start(), calls=%async_computation.4 | async-start | bytes 1064960 | tf_op jit(solution)/shard_map/all_gather | solution.py:17
  577.0 37.3 %collective-permute-start.15 = (f32[2048,128]{1,0:T(8,128)S(1)}, f32[2048,128]{1,0:T(8,128)S(1)}, u32[]{:S(2)}, u32[]{:S(2)}) collective-permute-start(f32[2048,128]{1,0:T(8,128)S(1)} %slice_select_fusion), channel_id=1, source_target_pairs={{0,256},{8,264},{16,272},{24,280},{32,288},{40,296},{48,304},{56,3... | collective-permute-start | bytes 3145736 | tf_op jit(solution)/shard_map/ppermute | solution.py:13
  614.5 43.3 %collective-permute-start.16 = (f32[1024,128]{1,0:T(8,128)S(1)}, f32[1024,128]{1,0:T(8,128)S(1)}, u32[]{:S(2)}, u32[]{:S(2)}) collective-permute-start(f32[1024,128]{1,0:T(8,128)S(1)} %slice_select_fusion.3), channel_id=1, source_target_pairs={{0,128},{8,136},{16,144},{24,152},{32,160},{40,168},{48,176},{56,1... | collective-permute-start | bytes 1572872 | tf_op jit(solution)/shard_map/ppermute | solution.py:13
  657.9 9.3 collective-permute-start.17
  667.3 7.2 collective-permute-start.18
  674.5 5.0 collective-permute-start.19
  679.6 6.4 collective-permute-start.20
  686.6 227.5 %all-gather.18.cloned.1.call-start = ((), (), s32[]{:S(2)}) async-start(), calls=%async_computation.5 | async-start | bytes 1064960 | tf_op jit(solution)/shard_map/all_gather | solution.py:17
  777.6 27.8 %collective-permute-start.21 = (f32[1024,128]{1,0:T(8,128)S(1)}, f32[1024,128]{1,0:T(8,128)S(1)}, u32[]{:S(2)}, u32[]{:S(2)}) collective-permute-start(f32[1024,128]{1,0:T(8,128)S(1)} %slice_select_fusion.2), channel_id=1, source_target_pairs={{0,128},{8,136},{16,144},{24,152},{32,160},{40,168},{48,176},{56,1... | collective-permute-start | bytes 1572872 | tf_op jit(solution)/shard_map/ppermute | solution.py:13
  805.5 113.0 %copy-start.1 = (bf16[64,1024]{1,0:T(8,128)(2,1)S(1)}, bf16[64,1024]{1,0:T(8,128)(2,1)}, u32[]{:S(2)}) copy-start(bf16[64,1024]{1,0:T(8,128)(2,1)} %copy-done) | copy-start | bytes 393220
  805.5 9.4 collective-permute-start.22
  815.0 7.2 collective-permute-start.23
  822.2 5.0 collective-permute-start.24
  827.3 6.4 collective-permute-start.25
  834.4 193.8 %all-gather.20.cloned.1.call-start = ((), (), s32[]{:S(2)}) async-start(), calls=%async_computation.6 | async-start | bytes 1064960 | tf_op jit(solution)/shard_map/all_gather | solution.py:17
  918.5 112.0 %copy-start.3 = (bf16[64,512]{1,0:T(8,128)(2,1)S(1)}, bf16[64,512]{1,0:T(8,128)(2,1)}, u32[]{:S(2)}) copy-start(bf16[64,512]{1,0:T(8,128)(2,1)} %copy-done.2) | copy-start | bytes 196612
  918.5 112.0 %copy-start.5 = (bf16[64,512]{1,0:T(8,128)(2,1)S(1)}, bf16[64,512]{1,0:T(8,128)(2,1)}, u32[]{:S(2)}) copy-start(bf16[64,512]{1,0:T(8,128)(2,1)} %copy-done.4) | copy-start | bytes 196612
  918.5 112.0 %copy-start.8 = (bf16[128,64]{0,1:T(8,128)(2,1)S(1)}, bf16[128,64]{0,1:T(8,128)(2,1)}, u32[]{:S(2)}) copy-start(bf16[128,64]{0,1:T(8,128)(2,1)} %copy-done.7) | copy-start | bytes 49156
  919.1 9.5 collective-permute-start.26
  928.7 7.2 collective-permute-start.27
  935.9 5.0 collective-permute-start.28
  941.0 6.2 collective-permute-start.29
  1030.9 8.2 collective-permute-start.30
  1039.2 5.0 collective-permute-start.31
  1044.2 5.0 collective-permute-start.32
  (14 other events, 624.3 us)
Sparse Core Ops, SparseCore 0:
  11.3 87.8 all-gather.7
  136.4 80.1 all-gather.9
  286.7 79.5 all-gather.11
  495.3 79.5 all-gather.13
  686.7 79.4 all-gather.15
  834.5 79.6 all-gather.17
  947.9 80.1 all-gather.19
where the time goes:
time: 1060 us
  waiting for transfers between devices  676 us (64%)
  blocking collectives  148 us (14%)
  starting transfers between devices  145 us (14%)
  other arithmetic  46.2 us (4%)
  local copies, waits for them, and re-layouts  17.4 us (2%)
  between operations  15.2 us (1%)
    all_gather x7, waiting for transfers between devices, collect_rows(): gathered = lax.all_gather(own_block, 'leaf', axis=0, tiled=True)  418 us
    ppermute x33, waiting for transfers between devices, swapped(): return lax.ppermute(value, axis, pairs)  257 us
    ppermute x33, starting transfers between devices, swapped(): return lax.ppermute(value, axis, pairs)  145 us
    scatter-add x3, other arithmetic, body(): accumulated = accumulated.at[row_list].add(update)  27.6 us
    all_gather x1, blocking collectives, body(): lax.all_gather(inv_3, 'panel', axis=0, tiled=True)  25.9 us
    all_gather x1, blocking collectives, body(): lax.all_gather(inv_0, 'panel', axis=0, tiled=True)  22.4 us
  transfers between devices with their start and end apart: 40, of which 40 were waited for; matrix products, arithmetic and copies ran while one was open for 0% of the time, Pallas kernels for 0%

commit v1 on v0

--- a/solution.py
+++ b/solution.py
@@ -14,7 +14,9 @@
 
 
 def collect_rows(own_block, groups, front_rows):
-    gathered = lax.all_gather(own_block, "leaf", axis=0, tiled=True)
+    gathered = jnp.concatenate(
+        lax.all_to_all(jnp.stack([own_block] * lax.axis_size("leaf")), "leaf", 0, 0), axis=0
+    )
     row_start = lax.axis_index("leaf") // groups * front_rows
     return lax.dynamic_slice_in_dim(gathered, row_start, front_rows, 0)
 

time: 1060 us -> 777 us (0.73)
  waiting for transfers between devices: 676 us -> 310 us
  starting transfers between devices: 145 us -> 238 us
  between operations: 15.2 us -> 1.72 us
    all_gather x7 -> x0, waiting for transfers between devices: 418 us -> none  [collect_rows(): gathered = lax.all_gather(own_block, 'leaf', axis=0, tiled=True)]
    all_to_all x0 -> x7, waiting for transfers between devices: none -> 87.5 us  [collect_rows(): lax.all_to_all(jnp.stack([own_block] * lax.axis_size('leaf')), 'leaf', 0, 0)]
    all_to_all x0 -> x7, starting transfers between devices: none -> 55.5 us  [collect_rows(): lax.all_to_all(jnp.stack([own_block] * lax.axis_size('leaf')), 'leaf', 0, 0)]
    ppermute x33, starting transfers between devices: 145 us -> 182 us  [swapped(): return lax.ppermute(value, axis, pairs)]
    ppermute x33, waiting for transfers between devices: 257 us -> 222 us  [swapped(): return lax.ppermute(value, axis, pairs)]
  transfers between devices with their start and end apart: 40 -> 40, of which waited for: 40 -> 37; matrix products, arithmetic and copies ran while one was open for 0% -> 1% of each run, Pallas kernels for 0% -> 0%
where the time goes in v1:
time: 777 us; the launch traced here: 775 us
  waiting for transfers between devices  310 us (40%)
  starting transfers between devices  238 us (31%)
  blocking collectives  148 us (19%)
  other arithmetic  44.2 us (6%)
  local copies, waits for them, and re-layouts  25.6 us (3%)
  matrix products  7.86 us (1%)
    ppermute x33, waiting for transfers between devices, swapped(): return lax.ppermute(value, axis, pairs)  222 us
    ppermute x33, starting transfers between devices, swapped(): return lax.ppermute(value, axis, pairs)  182 us
    all_to_all x7, waiting for transfers between devices, collect_rows(): lax.all_to_all(jnp.stack([own_block] * lax.axis_size('leaf')), 'leaf', 0, 0)  87.5 us
    all_to_all x7, starting transfers between devices, collect_rows(): lax.all_to_all(jnp.stack([own_block] * lax.axis_size('leaf')), 'leaf', 0, 0)  55.5 us
    scatter-add x3, other arithmetic, body(): accumulated = accumulated.at[row_list].add(update)  27.6 us
    all_gather x1, blocking collectives, body(): lax.all_gather(inv_3, 'panel', axis=0, tiled=True)  26.8 us
    all_gather x1, blocking collectives, body(): lax.all_gather(inv_0, 'panel', axis=0, tiled=True)  22 us
    all_gather x1, blocking collectives, body(): lax.all_gather(inv_1, 'panel', axis=0, tiled=True)  20.6 us
  transfers between devices with their start and end apart: 40, of which 37 were waited for; matrix products, arithmetic and copies ran while one was open for 1% of the time, Pallas kernels for 0%

profile of v1, /device:TPU:1, one launch (start us, length us, event | category | flops | bytes accessed | tf_op | source)
XLA Modules:
  0.0 774.8 jit_solution(14272911442897763930)
XLA Ops:
  2.6 11.6 %all-to-all-start = ((bf16[64,64,128]{2,1,0:T(8,128)(2,1)}), bf16[64,64,128]{2,1,0:T(8,128)(2,1)S(1)}, u32[]{:S(2)}, u32[]{:S(2)}) async-start(bf16[64,64,128]{2,1,0:T(8,128)(2,1)} %stack.14), calls=%async_computation | async-start | bytes 2097152 | tf_op jit(solution)/shard_map/all_to_all | solution.py:18
  14.3 26.8 %all_gather.21 = bf16[64,512]{1,0:T(8,128)(2,1)S(1)} all-gather(bf16[8,512]{1,0:T(8,128)(2,1)} %param.27), channel_id=1, replica_groups=mesh['leaf'=64,'panel'=8] {'panel'}, dimensions={0}, use_global_device_ids=true | all-gather | bytes 73728 | tf_op jit(solution)/shard_map/all_gather | solution.py:75
  41.0 19.0 %all_gather.22 = bf16[64,512]{1,0:T(8,128)(2,1)S(1)} all-gather(bf16[8,512]{1,0:T(8,128)(2,1)} %param.30), channel_id=1, replica_groups=mesh['leaf'=64,'panel'=8] {'panel'}, dimensions={0}, use_global_device_ids=true | all-gather | bytes 73728 | tf_op jit(solution)/shard_map/all_gather | solution.py:78
  76.0 4.4 collective-permute-start.1
  88.3 16.0 %collective-permute-start.3 = (f32[64,128]{1,0:T(8,128)S(1)}, f32[64,128]{1,0:T(8,128)S(1)}, u32[]{:S(2)}, u32[]{:S(2)}) collective-permute-start(f32[64,128]{1,0:T(8,128)S(1)} %slice_select_fusion.32), channel_id=1, source_target_pairs={{0,8},{8,0},{16,24},{24,16},{32,40},{40,32},{48,56},{56,48},{64,72... | collective-permute-start | bytes 98312 | tf_op jit(solution)/shard_map/ppermute | solution.py:13
  106.4 10.2 %all-to-all-start.1 = ((bf16[64,64,128]{2,1,0:T(8,128)(2,1)}), bf16[64,64,128]{2,1,0:T(8,128)(2,1)S(1)}, u32[]{:S(2)}, u32[]{:S(2)}) async-start(bf16[64,64,128]{2,1,0:T(8,128)(2,1)} %stack.15), calls=%async_computation.1 | async-start | bytes 2097152 | tf_op jit(solution)/shard_map/all_to_all | solution.py:18
  116.7 20.3 %all_gather.23 = bf16[64,1024]{1,0:T(8,128)(2,1)S(1)} all-gather(bf16[8,1024]{1,0:T(8,128)(2,1)S(1)} %copy-done.18), channel_id=1, replica_groups=mesh['leaf'=64,'panel'=8] {'panel'}, dimensions={0}, use_global_device_ids=true | all-gather | bytes 147456 | tf_op jit(solution)/shard_map/all_gather | solution.py:74
  137.0 19.1 %all_gather.24 = bf16[64,1024]{1,0:T(8,128)(2,1)S(1)} all-gather(bf16[8,1024]{1,0:T(8,128)(2,1)S(1)} %copy-done.19), channel_id=1, replica_groups=mesh['leaf'=64,'panel'=8] {'panel'}, dimensions={0}, use_global_device_ids=true | all-gather | bytes 147456 | tf_op jit(solution)/shard_map/all_gather | solution.py:77
  158.1 9.3 %scatter_fusion = f32[7168,128]{1,0:T(8,128)} fusion(f32[7168,128]{1,0:T(8,128)} %scatter_custom_fusion, s32[1024]{0:T(1024)S(1)} %bitcast.60, f32[1024,128]{1,0:T(8,128)S(1)} %copy.63), kind=kCustom, calls=%fused_computation.4 | custom fusion | flops 131072 | bytes 1576960 | tf_op jit(solution)/shard_map/scatter-add | solution.py:101
  172.7 18.8 %collective-permute-done.4 = f32[1024,128]{1,0:T(8,128)S(1)} collective-permute-done((f32[1024,128]{1,0:T(8,128)S(1)}, f32[1024,128]{1,0:T(8,128)S(1)}, u32[]{:S(2)}, u32[]{:S(2)}) %collective-permute-start.4) | collective-permute-done | bytes 524320 | tf_op jit(solution)/shard_map/ppermute | solution.py:13
  195.0 5.0 collective-permute-done.5
  200.1 4.9 collective-permute-start.6
  212.4 11.5 %collective-permute-start.8 = (f32[64,128]{1,0:T(8,128)S(1)}, f32[64,128]{1,0:T(8,128)S(1)}, u32[]{:S(2)}, u32[]{:S(2)}) collective-permute-start(f32[64,128]{1,0:T(8,128)S(1)} %slice_select_fusion.31), channel_id=1, source_target_pairs={{0,8},{8,0},{16,24},{24,16},{32,40},{40,32},{48,56},{56,48},{64,72... | collective-permute-start | bytes 98312 | tf_op jit(solution)/shard_map/ppermute | solution.py:13
  226.0 9.0 %all-to-all-start.2 = ((bf16[64,64,128]{2,1,0:T(8,128)(2,1)}), bf16[64,64,128]{2,1,0:T(8,128)(2,1)S(1)}, u32[]{:S(2)}, u32[]{:S(2)}) async-start(bf16[64,64,128]{2,1,0:T(8,128)(2,1)} %stack.16), calls=%async_computation.2 | async-start | bytes 2097152 | tf_op jit(solution)/shard_map/all_to_all | solution.py:18
  235.1 20.6 %all_gather.25 = bf16[64,2048]{1,0:T(8,128)(2,1)S(1)} all-gather(bf16[8,2048]{1,0:T(8,128)(2,1)S(1)} %copy-done.15), channel_id=1, replica_groups=mesh['leaf'=64,'panel'=8] {'panel'}, dimensions={0}, use_global_device_ids=true | all-gather | bytes 294912 | tf_op jit(solution)/shard_map/all_gather | solution.py:73
  255.6 20.0 %all_gather.26 = bf16[64,2048]{1,0:T(8,128)(2,1)S(1)} all-gather(bf16[8,2048]{1,0:T(8,128)(2,1)S(1)} %copy-done.16), channel_id=1, replica_groups=mesh['leaf'=64,'panel'=8] {'panel'}, dimensions={0}, use_global_device_ids=true | all-gather | bytes 294912 | tf_op jit(solution)/shard_map/all_gather | solution.py:76
  277.1 14.1 %scatter_fusion.1 = f32[7168,128]{1,0:T(8,128)} fusion(f32[7168,128]{1,0:T(8,128)} %scatter_fusion, s32[2048]{0:T(1024)S(1)} %bitcast.58, f32[2048,128]{1,0:T(8,128)S(1)} %copy.64), kind=kCustom, calls=%fused_computation.5 | custom fusion | flops 262144 | bytes 3153920 | tf_op jit(solution)/shard_map/scatter-add | solution.py:101
  293.0 6.4 collective-permute-start.9
  299.3 20.0 %collective-permute-done.9 = f32[2048,128]{1,0:T(8,128)S(1)} collective-permute-done((f32[2048,128]{1,0:T(8,128)S(1)}, f32[2048,128]{1,0:T(8,128)S(1)}, u32[]{:S(2)}, u32[]{:S(2)}) %collective-permute-start.9) | collective-permute-done | bytes 1048608 | tf_op jit(solution)/shard_map/ppermute | solution.py:13
  321.1 28.8 %collective-permute-start.10 = (f32[1024,128]{1,0:T(8,128)S(1)}, f32[1024,128]{1,0:T(8,128)S(1)}, u32[]{:S(2)}, u32[]{:S(2)}) collective-permute-start(f32[1024,128]{1,0:T(8,128)S(1)} %slice_select_fusion.4), channel_id=1, source_target_pairs={{0,128},{8,136},{16,144},{24,152},{32,160},{40,168},{48,176},{56,1... | collective-permute-start | bytes 1572872 | tf_op jit(solution)/shard_map/ppermute | solution.py:13
  349.9 22.6 %collective-permute-done.10 = f32[1024,128]{1,0:T(8,128)S(1)} collective-permute-done((f32[1024,128]{1,0:T(8,128)S(1)}, f32[1024,128]{1,0:T(8,128)S(1)}, u32[]{:S(2)}, u32[]{:S(2)}) %collective-permute-start.10) | collective-permute-done | bytes 524320 | tf_op jit(solution)/shard_map/ppermute | solution.py:13
  374.5 7.3 collective-permute-done.11
  383.9 5.3 collective-permute-done.12
  394.2 5.6 collective-permute-start.14
  401.9 6.7 all-to-all-start.3
  408.7 22.0 %all_gather.27 = bf16[64,4096]{1,0:T(8,128)(2,1)S(1)} all-gather(bf16[8,4096]{1,0:T(8,128)(2,1)S(1)} %copy-done.12), channel_id=1, replica_groups=mesh['leaf'=64,'panel'=8] {'panel'}, dimensions={0}, use_global_device_ids=true | all-gather | bytes 589824 | tf_op jit(solution)/shard_map/all_gather | solution.py:72
  430.7 6.1 all-to-all-done.3
  443.6 37.0 %collective-permute-done.15 = f32[2048,128]{1,0:T(8,128)S(1)} collective-permute-done((f32[2048,128]{1,0:T(8,128)S(1)}, f32[2048,128]{1,0:T(8,128)S(1)}, u32[]{:S(2)}, u32[]{:S(2)}) %collective-permute-start.15) | collective-permute-done | bytes 1048608 | tf_op jit(solution)/shard_map/ppermute | solution.py:13
  480.9 13.5 %collective-permute-start.16 = (f32[1024,128]{1,0:T(8,128)S(1)}, f32[1024,128]{1,0:T(8,128)S(1)}, u32[]{:S(2)}, u32[]{:S(2)}) collective-permute-start(f32[1024,128]{1,0:T(8,128)S(1)} %slice_select_fusion.3), channel_id=1, source_target_pairs={{0,128},{8,136},{16,144},{24,152},{32,160},{40,168},{48,176},{56,1... | collective-permute-start | bytes 1572872 | tf_op jit(solution)/shard_map/ppermute | solution.py:13
  494.4 21.5 %collective-permute-done.16 = f32[1024,128]{1,0:T(8,128)S(1)} collective-permute-done((f32[1024,128]{1,0:T(8,128)S(1)}, f32[1024,128]{1,0:T(8,128)S(1)}, u32[]{:S(2)}, u32[]{:S(2)}) %collective-permute-start.16) | collective-permute-done | bytes 524320 | tf_op jit(solution)/shard_map/ppermute | solution.py:13
  516.0 4.5 collective-permute-start.17
  520.5 5.1 collective-permute-done.17
  533.0 7.0 collective-permute-start.19
  541.7 5.3 collective-permute-start.20
  549.1 6.2 all-to-all-start.4
  556.5 27.0 %all-to-all-done.4 = bf16[64,64,128]{2,1,0:T(8,128)(2,1)S(1)} async-done(((bf16[64,64,128]{2,1,0:T(8,128)(2,1)}), bf16[64,64,128]{2,1,0:T(8,128)(2,1)S(1)}, u32[]{:S(2)}, u32[]{:S(2)}) %all-to-all-start.4) | async-done | bytes 1048608 | tf_op jit(solution)/shard_map/all_to_all | solution.py:18
  583.6 8.7 %gather_fusion = bf16[2048,128]{1,0:T(8,128)(2,1)} fusion(bf16[7168,128]{1,0:T(8,128)(2,1)S(1)} %scatter.10, s32[2048]{0:T(1024)} %broadcast_clamp_fusion), kind=kCustom, calls=%fused_computation | custom fusion | bytes 1056768 | tf_op jit(solution)/shard_map/jit(_take)/gather | solution.py:110
  596.7 24.5 %collective-permute-done.21 = f32[1024,128]{1,0:T(8,128)S(1)} collective-permute-done((f32[1024,128]{1,0:T(8,128)S(1)}, f32[1024,128]{1,0:T(8,128)S(1)}, u32[]{:S(2)}, u32[]{:S(2)}) %collective-permute-start.21) | collective-permute-done | bytes 524320 | tf_op jit(solution)/shard_map/ppermute | solution.py:13
  623.2 6.4 collective-permute-done.22
  629.7 4.3 collective-permute-start.23
  642.0 6.5 collective-permute-start.25
  650.6 6.1 all-to-all-start.5
  657.3 27.6 %all-to-all-done.5 = bf16[64,64,128]{2,1,0:T(8,128)(2,1)S(1)} async-done(((bf16[64,64,128]{2,1,0:T(8,128)(2,1)}), bf16[64,64,128]{2,1,0:T(8,128)(2,1)S(1)}, u32[]{:S(2)}, u32[]{:S(2)}) %all-to-all-start.5) | async-done | bytes 1048608 | tf_op jit(solution)/shard_map/all_to_all | solution.py:18
  692.8 5.5 collective-permute-done.26
  710.7 6.2 collective-permute-start.29
  719.0 5.7 all-to-all-start.6
  726.1 26.8 %all-to-all-done.6 = bf16[64,64,128]{2,1,0:T(8,128)(2,1)S(1)} async-done(((bf16[64,64,128]{2,1,0:T(8,128)(2,1)}), bf16[64,64,128]{2,1,0:T(8,128)(2,1)S(1)}, u32[]{:S(2)}, u32[]{:S(2)}) %all-to-all-start.6) | async-done | bytes 1048608 | tf_op jit(solution)/shard_map/all_to_all | solution.py:18
  768.0 5.4 collective-permute-start.32
  (195 shorter events, 141.1 us)
Async XLA Ops:
  2.6 58.7 %all-to-all-start = ((bf16[64,64,128]{2,1,0:T(8,128)(2,1)}), bf16[64,64,128]{2,1,0:T(8,128)(2,1)S(1)}, u32[]{:S(2)}, u32[]{:S(2)}) async-start(bf16[64,64,128]{2,1,0:T(8,128)(2,1)} %stack.14), calls=%async_computation | async-start | bytes 2097152 | tf_op jit(solution)/shard_map/all_to_all | solution.py:18
  66.7 50.0 %copy-start.18 = (bf16[8,1024]{1,0:T(8,128)(2,1)S(1)}, bf16[8,1024]{1,0:T(8,128)(2,1)}, u32[]{:S(2)}) copy-start(bf16[8,1024]{1,0:T(8,128)(2,1)} %param.26) | copy-start | bytes 49156
  66.7 70.3 %copy-start.19 = (bf16[8,1024]{1,0:T(8,128)(2,1)S(1)}, bf16[8,1024]{1,0:T(8,128)(2,1)}, u32[]{:S(2)}) copy-start(bf16[8,1024]{1,0:T(8,128)(2,1)} %param.29) | copy-start | bytes 49156
  67.8 7.1 collective-permute-start
  76.0 7.2 collective-permute-start.1
  83.3 5.0 collective-permute-start.2
  88.3 16.8 %collective-permute-start.3 = (f32[64,128]{1,0:T(8,128)S(1)}, f32[64,128]{1,0:T(8,128)S(1)}, u32[]{:S(2)}, u32[]{:S(2)}) collective-permute-start(f32[64,128]{1,0:T(8,128)S(1)} %slice_select_fusion.32), channel_id=1, source_target_pairs={{0,8},{8,0},{16,24},{24,16},{32,40},{40,32},{48,56},{56,48},{64,72... | collective-permute-start | bytes 98312 | tf_op jit(solution)/shard_map/ppermute | solution.py:13
  106.4 51.0 %all-to-all-start.1 = ((bf16[64,64,128]{2,1,0:T(8,128)(2,1)}), bf16[64,64,128]{2,1,0:T(8,128)(2,1)S(1)}, u32[]{:S(2)}, u32[]{:S(2)}) async-start(bf16[64,64,128]{2,1,0:T(8,128)(2,1)} %stack.15), calls=%async_computation.1 | async-start | bytes 2097152 | tf_op jit(solution)/shard_map/all_to_all | solution.py:18
  167.3 57.4 %copy-start.22 = (bf16[64,128]{1,0:T(8,128)(2,1)S(1)}, bf16[64,128]{1,0:T(8,128)(2,1)}, u32[]{:S(2)}) copy-start(bf16[64,128]{1,0:T(8,128)(2,1)} %param.21) | copy-start | bytes 49156
  168.6 22.9 %collective-permute-start.4 = (f32[1024,128]{1,0:T(8,128)S(1)}, f32[1024,128]{1,0:T(8,128)S(1)}, u32[]{:S(2)}, u32[]{:S(2)}) collective-permute-start(f32[1024,128]{1,0:T(8,128)S(1)} %slice_select_fusion.5), channel_id=1, source_target_pairs={{0,128},{8,136},{16,144},{24,152},{32,160},{40,168},{48,176},{56,1... | collective-permute-start | bytes 1572872 | tf_op jit(solution)/shard_map/ppermute | solution.py:13
  192.8 62.8 %copy-start.16 = (bf16[8,2048]{1,0:T(8,128)(2,1)S(1)}, bf16[8,2048]{1,0:T(8,128)(2,1)}, u32[]{:S(2)}) copy-start(bf16[8,2048]{1,0:T(8,128)(2,1)} %param.28) | copy-start | bytes 98308
  192.9 82.8 %copy-start.25 = (s32[2,2048]{1,0:T(2,128)S(1)}, s32[2,2048]{1,0:T(2,128)}, u32[]{:S(2)}) copy-start(s32[2,2048]{1,0:T(2,128)} %param.31) | copy-start | bytes 49156
  192.9 7.1 collective-permute-start.5
  200.1 7.3 collective-permute-start.6
  207.4 5.0 collective-permute-start.7
  212.4 12.3 %collective-permute-start.8 = (f32[64,128]{1,0:T(8,128)S(1)}, f32[64,128]{1,0:T(8,128)S(1)}, u32[]{:S(2)}, u32[]{:S(2)}) collective-permute-start(f32[64,128]{1,0:T(8,128)S(1)} %slice_select_fusion.31), channel_id=1, source_target_pairs={{0,8},{8,0},{16,24},{24,16},{32,40},{40,32},{48,56},{56,48},{64,72... | collective-permute-start | bytes 98312 | tf_op jit(solution)/shard_map/ppermute | solution.py:13
  226.0 50.2 %all-to-all-start.2 = ((bf16[64,64,128]{2,1,0:T(8,128)(2,1)}), bf16[64,64,128]{2,1,0:T(8,128)(2,1)S(1)}, u32[]{:S(2)}, u32[]{:S(2)}) async-start(bf16[64,64,128]{2,1,0:T(8,128)(2,1)} %stack.16), calls=%async_computation.2 | async-start | bytes 2097152 | tf_op jit(solution)/shard_map/all_to_all | solution.py:18
  293.0 26.4 %collective-permute-start.9 = (f32[2048,128]{1,0:T(8,128)S(1)}, f32[2048,128]{1,0:T(8,128)S(1)}, u32[]{:S(2)}, u32[]{:S(2)}) collective-permute-start(f32[2048,128]{1,0:T(8,128)S(1)} %slice_select_fusion.1), channel_id=1, source_target_pairs={{0,256},{8,264},{16,272},{24,280},{32,288},{40,296},{48,304},{56,3... | collective-permute-start | bytes 3145736 | tf_op jit(solution)/shard_map/ppermute | solution.py:13
  321.0 79.6 %copy-start.23 = (bf16[64,128]{1,0:T(8,128)(2,1)S(1)}, bf16[64,128]{1,0:T(8,128)(2,1)}, u32[]{:S(2)}) copy-start(bf16[64,128]{1,0:T(8,128)(2,1)} %param.20) | copy-start | bytes 49156
  321.1 51.4 %collective-permute-start.10 = (f32[1024,128]{1,0:T(8,128)S(1)}, f32[1024,128]{1,0:T(8,128)S(1)}, u32[]{:S(2)}, u32[]{:S(2)}) collective-permute-start(f32[1024,128]{1,0:T(8,128)S(1)} %slice_select_fusion.4), channel_id=1, source_target_pairs={{0,128},{8,136},{16,144},{24,152},{32,160},{40,168},{48,176},{56,1... | collective-permute-start | bytes 1572872 | tf_op jit(solution)/shard_map/ppermute | solution.py:13
  372.6 9.3 %collective-permute-start.11 = (f32[512,128]{1,0:T(8,128)S(1)}, f32[512,128]{1,0:T(8,128)S(1)}, u32[]{:S(2)}, u32[]{:S(2)}) collective-permute-start(f32[512,128]{1,0:T(8,128)S(1)} %slice_select_fusion.9), channel_id=1, source_target_pairs={{0,64},{8,72},{16,80},{24,88},{32,96},{40,104},{48,112},{56,120},{... | collective-permute-start | bytes 786440 | tf_op jit(solution)/shard_map/ppermute | solution.py:13
  381.9 7.2 collective-permute-start.12
  389.2 5.0 collective-permute-start.13
  394.2 6.4 collective-permute-start.14
  401.9 34.9 %all-to-all-start.3 = ((bf16[64,64,128]{2,1,0:T(8,128)(2,1)}), bf16[64,64,128]{2,1,0:T(8,128)(2,1)S(1)}, u32[]{:S(2)}, u32[]{:S(2)}) async-start(bf16[64,64,128]{2,1,0:T(8,128)(2,1)} %stack.17), calls=%async_computation.3 | async-start | bytes 2097152 | tf_op jit(solution)/shard_map/all_to_all | solution.py:18
  439.9 40.7 %collective-permute-start.15 = (f32[2048,128]{1,0:T(8,128)S(1)}, f32[2048,128]{1,0:T(8,128)S(1)}, u32[]{:S(2)}, u32[]{:S(2)}) collective-permute-start(f32[2048,128]{1,0:T(8,128)S(1)} %slice_select_fusion), channel_id=1, source_target_pairs={{0,256},{8,264},{16,272},{24,280},{32,288},{40,296},{48,304},{56,3... | collective-permute-start | bytes 3145736 | tf_op jit(solution)/shard_map/ppermute | solution.py:13
  480.9 35.0 %collective-permute-start.16 = (f32[1024,128]{1,0:T(8,128)S(1)}, f32[1024,128]{1,0:T(8,128)S(1)}, u32[]{:S(2)}, u32[]{:S(2)}) collective-permute-start(f32[1024,128]{1,0:T(8,128)S(1)} %slice_select_fusion.3), channel_id=1, source_target_pairs={{0,128},{8,136},{16,144},{24,152},{32,160},{40,168},{48,176},{56,1... | collective-permute-start | bytes 1572872 | tf_op jit(solution)/shard_map/ppermute | solution.py:13
  516.0 9.6 %collective-permute-start.17 = (f32[512,128]{1,0:T(8,128)S(1)}, f32[512,128]{1,0:T(8,128)S(1)}, u32[]{:S(2)}, u32[]{:S(2)}) collective-permute-start(f32[512,128]{1,0:T(8,128)S(1)} %slice_select_fusion.8), channel_id=1, source_target_pairs={{0,64},{8,72},{16,80},{24,88},{32,96},{40,104},{48,112},{56,120},{... | collective-permute-start | bytes 786440 | tf_op jit(solution)/shard_map/ppermute | solution.py:13
  525.7 7.2 collective-permute-start.18
  533.0 8.7 %collective-permute-start.19 = (f32[128,128]{1,0:T(8,128)S(1)}, f32[128,128]{1,0:T(8,128)S(1)}, u32[]{:S(2)}, u32[]{:S(2)}) collective-permute-start(f32[128,128]{1,0:T(8,128)S(1)} %slice_select_fusion.22), channel_id=1, source_target_pairs={{0,16},{8,24},{16,0},{24,8},{32,48},{40,56},{48,32},{56,40},{64,80... | collective-permute-start | bytes 196616 | tf_op jit(solution)/shard_map/ppermute | solution.py:13
  541.7 6.1 collective-permute-start.20
  549.1 34.3 %all-to-all-start.4 = ((bf16[64,64,128]{2,1,0:T(8,128)(2,1)}), bf16[64,64,128]{2,1,0:T(8,128)(2,1)S(1)}, u32[]{:S(2)}, u32[]{:S(2)}) async-start(bf16[64,64,128]{2,1,0:T(8,128)(2,1)} %stack.18), calls=%async_computation.4 | async-start | bytes 2097152 | tf_op jit(solution)/shard_map/all_to_all | solution.py:18
  594.2 26.9 %collective-permute-start.21 = (f32[1024,128]{1,0:T(8,128)S(1)}, f32[1024,128]{1,0:T(8,128)S(1)}, u32[]{:S(2)}, u32[]{:S(2)}) collective-permute-start(f32[1024,128]{1,0:T(8,128)S(1)} %slice_select_fusion.2), channel_id=1, source_target_pairs={{0,128},{8,136},{16,144},{24,152},{32,160},{40,168},{48,176},{56,1... | collective-permute-start | bytes 1572872 | tf_op jit(solution)/shard_map/ppermute | solution.py:13
  621.3 8.3 %collective-permute-start.22 = (f32[512,128]{1,0:T(8,128)S(1)}, f32[512,128]{1,0:T(8,128)S(1)}, u32[]{:S(2)}, u32[]{:S(2)}) collective-permute-start(f32[512,128]{1,0:T(8,128)S(1)} %slice_select_fusion.7), channel_id=1, source_target_pairs={{0,64},{8,72},{16,80},{24,88},{32,96},{40,104},{48,112},{56,120},{... | collective-permute-start | bytes 786440 | tf_op jit(solution)/shard_map/ppermute | solution.py:13
  629.7 7.2 collective-permute-start.23
  636.9 5.0 collective-permute-start.24
  642.0 7.4 collective-permute-start.25
  650.6 34.3 %all-to-all-start.5 = ((bf16[64,64,128]{2,1,0:T(8,128)(2,1)}), bf16[64,64,128]{2,1,0:T(8,128)(2,1)S(1)}, u32[]{:S(2)}, u32[]{:S(2)}) async-start(bf16[64,64,128]{2,1,0:T(8,128)(2,1)} %stack.19), calls=%async_computation.5 | async-start | bytes 2097152 | tf_op jit(solution)/shard_map/all_to_all | solution.py:18
  689.7 64.6 %copy-start.6 = (bf16[128,64]{0,1:T(8,128)(2,1)S(1)}, bf16[128,64]{0,1:T(8,128)(2,1)}, u32[]{:S(2)}) copy-start(bf16[128,64]{0,1:T(8,128)(2,1)} %copy-done.5) | copy-start | bytes 49156
  689.7 8.6 %collective-permute-start.26 = (f32[512,128]{1,0:T(8,128)S(1)}, f32[512,128]{1,0:T(8,128)S(1)}, u32[]{:S(2)}, u32[]{:S(2)}) collective-permute-start(f32[512,128]{1,0:T(8,128)S(1)} %slice_select_fusion.6), channel_id=1, source_target_pairs={{0,64},{8,72},{16,80},{24,88},{32,96},{40,104},{48,112},{56,120},{... | collective-permute-start | bytes 786440 | tf_op jit(solution)/shard_map/ppermute | solution.py:13
  698.4 7.2 collective-permute-start.27
  705.6 5.0 collective-permute-start.28
  710.7 7.1 collective-permute-start.29
  717.7 57.0 %copy-start.11 = (bf16[64,128]{1,0:T(8,128)(2,1)}, bf16[64,128]{1,0:T(8,128)(2,1)S(1)}, u32[]{:S(2)}) copy-start(bf16[64,128]{1,0:T(8,128)(2,1)S(1)} %add_convert_fusion.1) | copy-start | bytes 49156
  719.0 33.9 %all-to-all-start.6 = ((bf16[64,64,128]{2,1,0:T(8,128)(2,1)}), bf16[64,64,128]{2,1,0:T(8,128)(2,1)S(1)}, u32[]{:S(2)}, u32[]{:S(2)}) async-start(bf16[64,64,128]{2,1,0:T(8,128)(2,1)} %stack.20), calls=%async_computation.6 | async-start | bytes 2097152 | tf_op jit(solution)/shard_map/all_to_all | solution.py:18
  755.7 7.2 collective-permute-start.30
  762.9 5.0 collective-permute-start.31
  768.0 6.2 collective-permute-start.32
  (18 other events, 422.4 us)
